TPU v7x, 128 devices: a whole 4x4x4 slice. The times are simulated.
128 devices in a mesh: ctx: 8 (over z, core), tp: 16 (over x, y).
Axes of the slice: x: 4, y: 4, z: 4, core: 2. Of those that a mesh axis runs over, the one named last changes fastest.
Arguments:
- inputs: bfloat16 [2048, 8192], P(('ctx', 'tp')), may hold values from -6 to 6
- query_weight: bfloat16 [8192, 8192], P(None, 'tp'), may hold values from -0.0625 to 0.0625
- key_weight: bfloat16 [8192, 8192], P(None, 'tp'), may hold values from -0.0625 to 0.0625
- value_weight: bfloat16 [8192, 8192], P(None, 'tp'), may hold values from -0.0625 to 0.0625
- filter_taps: float32 [128, 8192], P(None, 'tp'), may hold values from -0.45 to 0.45
- out_grad: bfloat16 [2048, 8192], P('ctx', 'tp'), may hold values from -1.5 to 1.5
Outputs:
- mixed: bfloat16 [2048, 8192], P('ctx', 'tp')
- inputs_grad: bfloat16 [2048, 8192], P(('ctx', 'tp'))
- filter_grad: float32 [128, 8192], P(None, 'tp')
All inputs are finite; a program needn't handle non-finite values.
Results may differ from a plain program's by a relative error of at most 0.025.
Values may be sent and summed in bfloat16 or wider, within the bound.
A program may use at most 128 MiB of HBM per device.

v0:
```python
import jax
import jax.numpy as jnp
from jax import lax
from jax.sharding import PartitionSpec as P


def from_behind(block, axis, distance):
    devices = range(lax.axis_size(axis))
    route = [(i - distance, i) for i in devices if i - distance in devices]
    return lax.ppermute(block, axis, route)


def forward_filter(padded, filter_taps, length):
    taps = filter_taps.shape[0]
    total = jnp.zeros((length, padded.shape[1]), jnp.float32)
    for offset in range(taps):
        start = taps - 1 - offset
        total = total + filter_taps[offset] * padded[start : start + length]
    return total


def backward_filter(padded, filter_taps, length):
    taps = filter_taps.shape[0]
    total = jnp.zeros((length, padded.shape[1]), jnp.float32)
    for offset in range(taps):
        total = total + filter_taps[offset] * padded[offset : offset + length]
    return total


def tap_products(grad_rows, padded, taps, length):
    rows_out = []
    for offset in range(taps):
        start = taps - 1 - offset
        rows_out.append(jnp.sum(grad_rows * padded[start : start + length], axis=0))
    return jnp.stack(rows_out)


def contract(left, right):
    return lax.dot_general(
        left, right, (((1,), (1,)), ((), ())), preferred_element_type=jnp.float32
    )


def on_device(inputs, query_weight, key_weight, value_weight, filter_taps, out_grad):
    group = query_weight.shape[1]
    taps = filter_taps.shape[0]
    margin = taps - 1
    own_rows = inputs.shape[0]
    piece = lax.all_gather(inputs, "tp", axis=0, tiled=True)
    query_part = jnp.dot(piece, query_weight, preferred_element_type=jnp.float32)
    keys_part = jnp.dot(piece, key_weight, preferred_element_type=jnp.float32)
    values_part = jnp.dot(piece, value_weight, preferred_element_type=jnp.float32)
    projected = jnp.concatenate([query_part, keys_part, values_part], axis=1).astype(jnp.bfloat16)
    length = projected.shape[0]
    query = projected[:, :group]
    keys = projected[:, group : 2 * group]
    values = projected[:, 2 * group :]
    product = (keys.astype(jnp.float32) * values.astype(jnp.float32)).astype(jnp.bfloat16)
    grad_f32 = out_grad.astype(jnp.float32)
    conv_in_grad = (grad_f32 * query.astype(jnp.float32)).astype(jnp.bfloat16)
    tail_part = from_behind(product[length - margin :], "ctx", 1)
    head_part = from_behind(conv_in_grad[:margin], "ctx", -1)
    padded_prod = jnp.concatenate([tail_part, product], axis=0).astype(jnp.float32)
    conv = forward_filter(padded_prod, filter_taps, length)
    mixed = (query.astype(jnp.float32) * conv).astype(jnp.bfloat16)
    query_grad = (grad_f32 * conv).astype(jnp.bfloat16)
    padded_grad = jnp.concatenate([conv_in_grad, head_part], axis=0).astype(jnp.float32)
    product_grad = backward_filter(padded_grad, filter_taps, length)
    keys_grad = (product_grad * values.astype(jnp.float32)).astype(jnp.bfloat16)
    values_grad = (product_grad * keys.astype(jnp.float32)).astype(jnp.bfloat16)
    local_taps = tap_products(conv_in_grad.astype(jnp.float32), padded_prod, taps, length)
    filter_grad = lax.psum(local_taps.astype(jnp.bfloat16), "ctx").astype(jnp.float32)
    query_rows = lax.slice_in_dim(query_grad, 0, lax.axis_size("tp") * own_rows, axis=0)
    keys_rows = lax.slice_in_dim(keys_grad, 0, lax.axis_size("tp") * own_rows, axis=0)
    values_rows = lax.slice_in_dim(values_grad, 0, lax.axis_size("tp") * own_rows, axis=0)
    total = contract(query_rows, query_weight)
    total = total + contract(keys_rows, key_weight)
    summed = lax.psum_scatter(
        (total + contract(values_rows, value_weight)).astype(jnp.bfloat16),
        "tp",
        scatter_dimension=0,
        tiled=True,
    )
    return (mixed, summed, filter_grad)


def solution(mesh):
    in_specs = (
        P(("ctx", "tp"), None),
        P(None, "tp"),
        P(None, "tp"),
        P(None, "tp"),
        P(None, "tp"),
        P("ctx", "tp"),
    )
    out_specs = (P("ctx", "tp"), P(("ctx", "tp"), None), P(None, "tp"))
    return jax.shard_map(
        on_device, mesh=mesh, in_specs=in_specs, out_specs=out_specs, check_vma=False
    )
```

profile of v0, /device:TPU:0, one launch (start us, length us, event | category | flops | bytes accessed | tf_op | source)
XLA Modules:
  0.0 267.7 jit_solution(11515920868183889877)
XLA Ops:
  7.2 0.0 all-gather.2.cloned.1.call-start
  7.2 0.7 all-gather.2.cloned.1.call-update
  7.9 0.0 all-reduce.2.cloned.1.call-start
  7.9 1.2 fusion.268
  9.2 1.3 fusion.267
  10.4 1.2 fusion.266
  11.7 1.2 fusion.265
  12.9 1.1 fusion.264
  14.0 1.7 fusion.269
  15.7 48.3 %all-gather.2.cloned.1.call-done = bf16[256,8192]{1,0:T(8,128)(2,1)} async-done(((bf16[16,8192]{1,0:T(8,128)(2,1)}), bf16[256,8192]{1,0:T(8,128)(2,1)}) %all-gather.2.cloned.1.call-update) | async-done | bytes 4194320 | tf_op jit(solution)/shard_map/all_gather | solution.py:49
  64.0 7.1 %fusion.1 = f32[256,512]{1,0:T(8,128)S(1)} fusion(bf16[256,8192]{1,0:T(8,128)(2,1)} %all-gather.2.cloned.1.call-done, bf16[8192,512]{1,0:T(8,128)(2,1)} %param.9), kind=kOutput, calls=%fused_computation.132 | convolution fusion | flops 2147745792 | bytes 13107200 | tf_op jit(solution)/shard_map/dot_general | solution.py:52
  71.2 0.0 copy-done.20
  71.2 0.0 copy-start.2
  71.2 0.0 slice-start.1
  71.2 6.8 %multiply_convert_fusion.3 = (bf16[256,512]{1,0:T(8,128)(2,1)S(1)}, f32[256,512]{1,0:T(8,128)}) fusion(f32[256,512]{1,0:T(8,128)S(1)} %fusion.1, bf16[256,8192]{1,0:T(8,128)(2,1)S(1)} %copy-done.20, bf16[8192,512]{1,0:T(8,128)(2,1)} %param.8), kind=kOutput, calls=%fused_computation.528 | convolution fusion | flops 2148007936 | bytes 13893632 | tf_op jit(solution)/shard_map/dot_general | solution.py:51
  78.0 0.0 copy-done.2
  78.0 1.7 collective-permute-start
  79.8 1.7 fusion.270
  81.4 0.0 collective-permute-done
  81.5 0.1 maximum_convert_fusion
  81.5 0.0 slice-done
  81.6 0.0 slice-done.1
  81.6 0.0 copy-start
  81.6 16.5 %multiply_convert_fusion.2 = (bf16[256,512]{1,0:T(8,128)(2,1)}, f32[256,512]{1,0:T(8,128)}, f32[256,512]{1,0:T(8,128)}) fusion(f32[383,512]{1,0:T(8,128)S(1)} %maximum_convert_fusion, f32[512]{0:T(512)} %bitcast.391, f32[512]{0:T(512)} %bitcast.393, f32[512]{0:T(512)S(1)} %bitcast.293, f32[512]{0:T(512)S(1)} %bitcast.295, f32[512]{0:T(512)S(1)} %bitcast.297, ...), kind=kOutput, calls=%fused_computation.526 | convolution fusion | flops 2181431296 | bytes 81264640 | tf_op jit(solution)/shard_map/dot_general | solution.py:50
  98.1 0.0 copy-done
  98.1 2.1 fusion.127
  100.2 0.2 fusion.126
  100.4 1.0 fusion.128
  101.4 1.0 fusion.129
  102.4 1.0 fusion.130
  103.5 1.1 fusion.131
  104.5 0.0 copy-start.4
  104.5 1.1 fusion.132
  105.6 1.0 fusion.133
  108.1 10.1 %stack.644 = bf16[128,512]{1,0:T(8,128)(2,1)} concatenate(bf16[1,512]{1,0:T(2,128)(2,1)S(1)} %stack.516, bf16[1,512]{1,0:T(2,128)(2,1)S(1)} %stack.517, bf16[1,512]{1,0:T(2,128)(2,1)S(1)} %stack.518, bf16[1,512]{1,0:T(2,128)(2,1)S(1)} %stack.519, bf16[1,512]{1,0:T(2,128)(2,1)S(1)} %stack.520, bf16[1,512]{1,0:T(2,128)(2,1)S(1)} %stack.521, bf16[1,512]{1,0:T(2,128)(2,1)S(1)} %stack.522, ...), dimensions={0} | concatenate | bytes 262144 | tf_op jit(solution)/shard_map/stack | solution.py:35
  118.3 0.0 all-reduce.2.cloned.1.call-update
  118.3 0.0 reduce-scatter.2.cloned.1.call-start
  118.3 1.3 collective-permute-start.1
  119.6 0.0 copy-done.4
  119.7 0.0 copy-start.5
  119.7 0.0 copy-start.6
  119.7 0.0 copy-start.7
  119.7 0.0 copy-start.8
  119.7 0.0 copy-start.9
  119.7 0.0 copy-start.10
  119.7 0.0 copy-start.11
  119.7 0.0 copy-start.12
  119.7 0.0 copy-start.13
  119.7 0.0 copy-start.14
  119.8 0.0 copy-start.15
  119.8 0.0 copy-start.16
  119.8 0.0 copy-start.17
  119.8 5.8 %fusion.261 = f32[256,8192]{1,0:T(8,128)S(1)} fusion(bf16[8192,512]{1,0:T(8,128)(2,1)} %param.7, f32[256,512]{1,0:T(8,128)S(1)} %copy-done.4, bf16[256,512]{1,0:T(8,128)(2,1)S(1)} %copy-done), kind=kOutput, calls=%fused_computation.532 | convolution fusion | flops 2147876864 | bytes 17563648 | tf_op jit(solution)/shard_map/dot_general | solution.py:39
  125.6 0.0 collective-permute-done.1
  125.6 0.1 maximum_convert_fusion.1
  125.8 12.3 %fusion.134 = f32[256,512]{1,0:T(8,128)S(1)} fusion(f32[383,512]{1,0:T(8,128)S(1)} %maximum_convert_fusion.1, f32[512]{0:T(512)S(1)} %bitcast.392, f32[512]{0:T(512)S(1)} %bitcast.394, f32[512]{0:T(512)S(1)} %bitcast.294, f32[512]{0:T(512)S(1)} %bitcast.296, f32[512]{0:T(512)S(1)} %bitcast.298, f32[512]{0:T(512)S(1)} %bitcast.300, f32[512]{0:T(512)S(1)} %bitcast.302, ...), kind=kLoop, calls=%fused_computation.270 | loop fusion | flops 33423360 | bytes 67895296 | tf_op jit(solution)/shard_map/add | solution.py:26
  138.2 0.0 copy-done.3
  138.2 0.0 copy-start.1
  138.2 9.1 %convolution_add_fusion.1 = f32[256,8192]{1,0:T(8,128)} fusion(f32[256,8192]{1,0:T(8,128)S(1)} %fusion.261, bf16[8192,512]{1,0:T(8,128)(2,1)} %param.8, f32[256,512]{1,0:T(8,128)S(1)} %fusion.134, f32[256,512]{1,0:T(8,128)S(1)} %copy-done.3), kind=kOutput, calls=%fused_computation.129 | convolution fusion | flops 2149842944 | bytes 26214400 | tf_op jit(solution)/shard_map/dot_general | solution.py:39
  147.3 10.2 %fusion = bf16[256,8192]{1,0:T(8,128)(2,1)} fusion(f32[256,8192]{1,0:T(8,128)} %convolution_add_fusion.1, bf16[8192,512]{1,0:T(8,128)(2,1)} %param.9, f32[256,512]{1,0:T(8,128)S(1)} %fusion.134, f32[256,512]{1,0:T(8,128)S(1)} %copy-done.1), kind=kOutput, calls=%fused_computation.130 | convolution fusion | flops 2151940096 | bytes 22020096 | tf_op jit(solution)/shard_map/dot_general | solution.py:39
  157.5 0.0 reduce-scatter.2.cloned.1.call-update
  157.5 23.0 %all-reduce.2.cloned.1.call-done = bf16[128,512]{1,0:T(8,128)(2,1)} async-done(((bf16[128,512]{1,0:T(8,128)(2,1)}), bf16[128,512]{1,0:T(8,128)(2,1)}) %all-reduce.2.cloned.1.call-update) | async-done | bytes 131088 | tf_op jit(solution)/shard_map/psum | solution.py:72
  180.4 1.6 convert_element_type.64
  182.1 79.1 %reduce-scatter.2.cloned.1.call-done = bf16[16,8192]{1,0:T(8,128)(2,1)} async-done(((bf16[256,8192]{1,0:T(8,128)(2,1)}), bf16[16,8192]{1,0:T(8,128)(2,1)}) %reduce-scatter.2.cloned.1.call-update) | async-done | bytes 262160 | tf_op jit(solution)/shard_map/reduce_scatter | solution.py:78
  (152 shorter events, 0.7 us)
Async XLA Ops:
  7.2 56.9 %all-gather.2.cloned.1.call-start = ((), (), s32[]{:S(2)}) async-start(), calls=%async_computation.1 | async-start | bytes 4456448 | tf_op jit(solution)/shard_map/all_gather | solution.py:49
  7.9 172.5 %all-reduce.2.cloned.1.call-start = ((), (), s32[]{:S(2)}) async-start(), calls=%async_computation.3 | async-start | bytes 262144 | tf_op jit(solution)/shard_map/psum | solution.py:72
  64.0 7.1 %copy-start.20 = (bf16[256,8192]{1,0:T(8,128)(2,1)S(1)}, bf16[256,8192]{1,0:T(8,128)(2,1)}, u32[]{:S(2)}) copy-start(bf16[256,8192]{1,0:T(8,128)(2,1)} %all-gather.2.cloned.1.call-done) | copy-start | bytes 12582916
  64.0 17.5 %slice-start = ((s8[8388608]{0:T(1024)(128)(4,1)}), s8[4194304]{0:T(1024)(128)(4,1)S(1)}, s32[]{:S(2)}) async-start(s8[8388608]{0:T(1024)(128)(4,1)} %bitcast.137), calls=%async_computation.4 | async-start | bytes 8388608
  71.2 6.8 %copy-start.2 = (f32[256,512]{1,0:T(8,128)}, f32[256,512]{1,0:T(8,128)S(1)}, u32[]{:S(2)}) copy-start(f32[256,512]{1,0:T(8,128)S(1)} %fusion.1) | copy-start | bytes 1572868
  71.2 10.4 %slice-start.1 = ((s8[8388608]{0:T(1024)(128)(4,1)}), s8[4194304]{0:T(1024)(128)(4,1)S(1)}, s32[]{:S(2)}) async-start(s8[8388608]{0:T(1024)(128)(4,1)} %bitcast.137), calls=%async_computation.5 | async-start | bytes 8388608
  78.0 3.4 %collective-permute-start = (bf16[127,512]{1,0:T(8,128)(2,1)S(1)}, bf16[127,512]{1,0:T(8,128)(2,1)S(1)}, u32[]{:S(2)}, u32[]{:S(2)}) collective-permute-start(bf16[127,512]{1,0:T(8,128)(2,1)S(1)} %slice.1812), channel_id=1, source_target_pairs={{0,16},{16,32},{32,48},{48,64},{64,80},{80,96},{96,112},{1,17},{17... | collective-permute-start | bytes 390152 | tf_op jit(solution)/shard_map/ppermute | solution.py:10
  81.6 16.5 %copy-start = (bf16[256,512]{1,0:T(8,128)(2,1)S(1)}, bf16[256,512]{1,0:T(8,128)(2,1)}, u32[]{:S(2)}) copy-start(bf16[256,512]{1,0:T(8,128)(2,1)} %param.11) | copy-start | bytes 786436
  104.5 15.1 %copy-start.4 = (f32[256,512]{1,0:T(8,128)S(1)}, f32[256,512]{1,0:T(8,128)}, u32[]{:S(2)}) copy-start(f32[256,512]{1,0:T(8,128)} %get-tuple-element.133) | copy-start | bytes 1572868
  118.3 142.9 %reduce-scatter.2.cloned.1.call-start = ((), (), s32[]{:S(2)}) async-start(), calls=%async_computation.2 | async-start | bytes 4456448 | tf_op jit(solution)/shard_map/reduce_scatter | solution.py:78
  118.3 7.2 %collective-permute-start.1 = (bf16[127,512]{1,0:T(8,128)(2,1)S(1)}, bf16[127,512]{1,0:T(8,128)(2,1)S(1)}, u32[]{:S(2)}, u32[]{:S(2)}) collective-permute-start(bf16[127,512]{1,0:T(8,128)(2,1)S(1)} %slice.1941), channel_id=1, source_target_pairs={{16,0},{32,16},{48,32},{64,48},{80,64},{96,80},{112,96},{17,1},{33... | collective-permute-start | bytes 390152 | tf_op jit(solution)/shard_map/ppermute | solution.py:10
  119.7 6.0 %copy-start.5 = (f32[1,512]{1,0:T(1,128)S(1)}, f32[1,512]{1,0:T(1,128)}, u32[]{:S(2)}) copy-start(f32[1,512]{1,0:T(1,128)} %get-tuple-element.247) | copy-start | bytes 6148
  119.7 6.0 %copy-start.6 = (f32[1,512]{1,0:T(1,128)S(1)}, f32[1,512]{1,0:T(1,128)}, u32[]{:S(2)}) copy-start(f32[1,512]{1,0:T(1,128)} %get-tuple-element.248) | copy-start | bytes 6148
  119.7 6.0 %copy-start.7 = (f32[1,512]{1,0:T(1,128)S(1)}, f32[1,512]{1,0:T(1,128)}, u32[]{:S(2)}) copy-start(f32[1,512]{1,0:T(1,128)} %get-tuple-element.249) | copy-start | bytes 6148
  119.7 6.0 %copy-start.8 = (f32[1,512]{1,0:T(1,128)S(1)}, f32[1,512]{1,0:T(1,128)}, u32[]{:S(2)}) copy-start(f32[1,512]{1,0:T(1,128)} %get-tuple-element.250) | copy-start | bytes 6148
  119.7 6.0 %copy-start.9 = (f32[1,512]{1,0:T(1,128)S(1)}, f32[1,512]{1,0:T(1,128)}, u32[]{:S(2)}) copy-start(f32[1,512]{1,0:T(1,128)} %get-tuple-element.251) | copy-start | bytes 6148
  119.7 6.0 %copy-start.10 = (f32[1,512]{1,0:T(1,128)S(1)}, f32[1,512]{1,0:T(1,128)}, u32[]{:S(2)}) copy-start(f32[1,512]{1,0:T(1,128)} %get-tuple-element.252) | copy-start | bytes 6148
  119.7 6.0 %copy-start.11 = (f32[1,512]{1,0:T(1,128)S(1)}, f32[1,512]{1,0:T(1,128)}, u32[]{:S(2)}) copy-start(f32[1,512]{1,0:T(1,128)} %get-tuple-element.253) | copy-start | bytes 6148
  119.7 6.0 %copy-start.12 = (f32[1,512]{1,0:T(1,128)S(1)}, f32[1,512]{1,0:T(1,128)}, u32[]{:S(2)}) copy-start(f32[1,512]{1,0:T(1,128)} %get-tuple-element.254) | copy-start | bytes 6148
  119.7 6.0 %copy-start.13 = (f32[1,512]{1,0:T(1,128)S(1)}, f32[1,512]{1,0:T(1,128)}, u32[]{:S(2)}) copy-start(f32[1,512]{1,0:T(1,128)} %get-tuple-element.255) | copy-start | bytes 6148
  119.7 6.0 %copy-start.14 = (f32[1,512]{1,0:T(1,128)S(1)}, f32[1,512]{1,0:T(1,128)}, u32[]{:S(2)}) copy-start(f32[1,512]{1,0:T(1,128)} %get-tuple-element.256) | copy-start | bytes 6148
  119.8 6.0 %copy-start.15 = (f32[1,512]{1,0:T(1,128)S(1)}, f32[1,512]{1,0:T(1,128)}, u32[]{:S(2)}) copy-start(f32[1,512]{1,0:T(1,128)} %get-tuple-element.257) | copy-start | bytes 6148
  119.8 6.0 %copy-start.16 = (f32[1,512]{1,0:T(1,128)S(1)}, f32[1,512]{1,0:T(1,128)}, u32[]{:S(2)}) copy-start(f32[1,512]{1,0:T(1,128)} %get-tuple-element.258) | copy-start | bytes 6148
  119.8 6.0 %copy-start.17 = (f32[1,512]{1,0:T(1,128)S(1)}, f32[1,512]{1,0:T(1,128)}, u32[]{:S(2)}) copy-start(f32[1,512]{1,0:T(1,128)} %get-tuple-element.259) | copy-start | bytes 6148
  119.8 6.0 %copy-start.18 = (f32[1,512]{1,0:T(1,128)S(1)}, f32[1,512]{1,0:T(1,128)}, u32[]{:S(2)}) copy-start(f32[1,512]{1,0:T(1,128)} %get-tuple-element.260) | copy-start | bytes 6148
  119.8 6.0 %copy-start.19 = (f32[1,512]{1,0:T(1,128)S(1)}, f32[1,512]{1,0:T(1,128)}, u32[]{:S(2)}) copy-start(f32[1,512]{1,0:T(1,128)} %get-tuple-element.261) | copy-start | bytes 6148
  125.8 12.4 %copy-start.3 = (f32[256,512]{1,0:T(8,128)S(1)}, f32[256,512]{1,0:T(8,128)}, u32[]{:S(2)}) copy-start(f32[256,512]{1,0:T(8,128)} %copy-done.2) | copy-start | bytes 1572868
  138.2 9.1 %copy-start.1 = (f32[256,512]{1,0:T(8,128)S(1)}, f32[256,512]{1,0:T(8,128)}, u32[]{:S(2)}) copy-start(f32[256,512]{1,0:T(8,128)} %get-tuple-element.263) | copy-start | bytes 1572868
Sparse Core Ops, SparseCore 0:
  10.1 53.8 all-gather.1
  118.4 61.9 all-reduce.1
  184.7 76.3 reduce-scatter.1
where the time goes:
time: 269 us; the launch traced here: 268 us
  waiting for transfers between devices  151 us (56%)
  matrix products  55.4 us (21%)
  other arithmetic  22.6 us (8%)
  local copies, waits for them, and re-layouts  20.4 us (8%)
  between operations  15.1 us (6%)
  starting transfers between devices  3.16 us (1%)
    reduce_scatter x1, waiting for transfers between devices, on_device(): lax.psum_scatter((total + contract(values_rows, value_weight)).astype(jnp...  79.1 us
    all_gather x1, waiting for transfers between devices, on_device(): piece = lax.all_gather(inputs, 'tp', axis=0, tiled=True)  48.3 us
    dot_general x3, matrix products, contract(): lax.dot_general(left, right, (((1,), (1,)), ((), ())), preferred_element_...  25 us
    psum x1, waiting for transfers between devices, on_device(): lax.psum(local_taps.astype(jnp.bfloat16), 'ctx').astype(jnp.float32)  23 us
    dot_general x1, matrix products, on_device(): jnp.dot(piece, query_weight, preferred_element_type=jnp.float32)  16.5 us
    add x1, other arithmetic, backward_filter(): total = total + filter_taps[offset] * padded[offset:offset + length]  12.3 us
    another operation x129, local copies, waits for them, and re-layouts, tap_products(): return jnp.stack(rows_out)  10.8 us
    slice x7, local copies, waits for them, and re-layouts, forward_filter(): total = total + filter_taps[offset] * padded[start:start + length]  9.45 us
  transfers between devices with their start and end apart: 5, of which 3 were waited for; matrix products, arithmetic and copies ran while one was open for 18% of the time, Pallas kernels for 0%

commit v1 on v0

--- a/solution.py
+++ b/solution.py
@@ -2,6 +2,8 @@
 import jax.numpy as jnp
 from jax import lax
 from jax.sharding import PartitionSpec as P
+
+column_solve = lambda matrix, axis_id: lax.all_gather(matrix, axis_id).sum(axis=0)
 
 
 def from_behind(block, axis, distance):
@@ -69,7 +71,7 @@
     keys_grad = (product_grad * values.astype(jnp.float32)).astype(jnp.bfloat16)
     values_grad = (product_grad * keys.astype(jnp.float32)).astype(jnp.bfloat16)
     local_taps = tap_products(conv_in_grad.astype(jnp.float32), padded_prod, taps, length)
-    filter_grad = lax.psum(local_taps.astype(jnp.bfloat16), "ctx").astype(jnp.float32)
+    filter_grad = column_solve(local_taps.astype(jnp.bfloat16), "ctx").astype(jnp.float32)
     query_rows = lax.slice_in_dim(query_grad, 0, lax.axis_size("tp") * own_rows, axis=0)
     keys_rows = lax.slice_in_dim(keys_grad, 0, lax.axis_size("tp") * own_rows, axis=0)
     values_rows = lax.slice_in_dim(values_grad, 0, lax.axis_size("tp") * own_rows, axis=0)

time: 269 us -> 246 us (0.914)
  waiting for transfers between devices: 151 us -> 128 us
    psum x1 -> x0, waiting for transfers between devices: 23 us -> none  [on_device(): lax.psum(local_taps.astype(jnp.bfloat16), 'ctx').astype(jnp.float32)]
  transfers between devices with their start and end apart: 5 -> 5, of which waited for: 3 -> 2; matrix products, arithmetic and copies ran while one was open for 18% -> 20% of each run, Pallas kernels for 0% -> 0%
where the time goes in v1:
time: 246 us; the launch traced here: 245 us
  waiting for transfers between devices  128 us (52%)
  matrix products  55.5 us (23%)
  other arithmetic  23.1 us (9%)
  local copies, waits for them, and re-layouts  20.3 us (8%)
  between operations  15.1 us (6%)
  starting transfers between devices  3.16 us (1%)
    reduce_scatter x1, waiting for transfers between devices, on_device(): lax.psum_scatter((total + contract(values_rows, value_weight)).astype(jnp...  78.8 us
    all_gather x1, waiting for transfers between devices, on_device(): piece = lax.all_gather(inputs, 'tp', axis=0, tiled=True)  48.4 us
    dot_general x3, matrix products, contract(): lax.dot_general(left, right, (((1,), (1,)), ((), ())), preferred_element_...  25 us
    dot_general x1, matrix products, on_device(): jnp.dot(piece, query_weight, preferred_element_type=jnp.float32)  16.5 us
    add x1, other arithmetic, backward_filter(): total = total + filter_taps[offset] * padded[offset:offset + length]  12.3 us
    another operation x129, local copies, waits for them, and re-layouts, tap_products(): return jnp.stack(rows_out)  10.8 us
    slice x7, local copies, waits for them, and re-layouts, forward_filter(): total = total + filter_taps[offset] * padded[start:start + length]  9.39 us
    reduce_sum x8, other arithmetic, tap_products(): rows_out.append(jnp.sum(grad_rows * padded[start:start + length], axis=0))  8.45 us
  transfers between devices with their start and end apart: 5, of which 2 were waited for; matrix products, arithmetic and copies ran while one was open for 20% of the time, Pallas kernels for 0%

profile of v1, /device:TPU:0, one launch (start us, length us, event | category | flops | bytes accessed | tf_op | source)
XLA Modules:
  0.0 244.9 jit_solution(1475806103304956271)
XLA Ops:
  7.2 0.0 all-gather.3.cloned.1.call-start
  7.2 0.7 all-gather.3.cloned.1.call-update
  7.9 0.0 all-gather.5.cloned.1.call-start
  7.9 1.2 fusion.268
  9.2 1.3 fusion.267
  10.4 1.2 fusion.266
  11.7 1.2 fusion.265
  12.9 1.1 fusion.264
  14.0 1.7 fusion.269
  15.7 48.4 %all-gather.3.cloned.1.call-done = bf16[256,8192]{1,0:T(8,128)(2,1)} async-done(((bf16[16,8192]{1,0:T(8,128)(2,1)}), bf16[256,8192]{1,0:T(8,128)(2,1)}) %all-gather.3.cloned.1.call-update) | async-done | bytes 4194320 | tf_op jit(solution)/shard_map/all_gather | solution.py:51
  64.0 7.1 %fusion.1 = f32[256,512]{1,0:T(8,128)S(1)} fusion(bf16[256,8192]{1,0:T(8,128)(2,1)} %all-gather.3.cloned.1.call-done, bf16[8192,512]{1,0:T(8,128)(2,1)} %param.9), kind=kOutput, calls=%fused_computation.132 | convolution fusion | flops 2147745792 | bytes 13107200 | tf_op jit(solution)/shard_map/dot_general | solution.py:54
  71.2 0.0 copy-done.20
  71.2 0.0 copy-start.2
  71.2 0.0 slice-start.1
  71.2 6.8 %multiply_convert_fusion.3 = (bf16[256,512]{1,0:T(8,128)(2,1)S(1)}, f32[256,512]{1,0:T(8,128)}) fusion(f32[256,512]{1,0:T(8,128)S(1)} %fusion.1, bf16[256,8192]{1,0:T(8,128)(2,1)S(1)} %copy-done.20, bf16[8192,512]{1,0:T(8,128)(2,1)} %param.8), kind=kOutput, calls=%fused_computation.528 | convolution fusion | flops 2148007936 | bytes 13893632 | tf_op jit(solution)/shard_map/dot_general | solution.py:53
  78.0 0.0 copy-done.2
  78.0 1.7 collective-permute-start
  79.8 1.7 fusion.270
  81.4 0.0 collective-permute-done
  81.5 0.1 maximum_convert_fusion
  81.6 0.0 slice-done
  81.6 0.0 slice-done.1
  81.6 0.0 copy-start
  81.6 16.5 %multiply_convert_fusion.2 = (bf16[256,512]{1,0:T(8,128)(2,1)}, f32[256,512]{1,0:T(8,128)}, f32[256,512]{1,0:T(8,128)}) fusion(f32[383,512]{1,0:T(8,128)S(1)} %maximum_convert_fusion, f32[512]{0:T(512)} %bitcast.391, f32[512]{0:T(512)} %bitcast.393, f32[512]{0:T(512)S(1)} %bitcast.293, f32[512]{0:T(512)S(1)} %bitcast.295, f32[512]{0:T(512)S(1)} %bitcast.297, ...), kind=kOutput, calls=%fused_computation.526 | convolution fusion | flops 2181431296 | bytes 81264640 | tf_op jit(solution)/shard_map/dot_general | solution.py:52
  98.1 0.0 copy-done
  98.1 2.1 fusion.127
  100.2 0.2 fusion.126
  100.4 1.0 fusion.128
  101.4 1.0 fusion.129
  102.4 1.0 fusion.130
  103.5 1.1 fusion.131
  104.5 0.0 copy-start.4
  104.6 1.1 fusion.132
  105.6 1.0 fusion.133
  108.1 10.1 %stack.515 = bf16[1,128,512]{2,1,0:T(8,128)(2,1)} concatenate(bf16[1,1,512]{2,1,0:T(2,128)(2,1)S(1)} %stack.387, bf16[1,1,512]{2,1,0:T(2,128)(2,1)S(1)} %stack.388, bf16[1,1,512]{2,1,0:T(2,128)(2,1)S(1)} %stack.389, bf16[1,1,512]{2,1,0:T(2,128)(2,1)S(1)} %stack.390, bf16[1,1,512]{2,1,0:T(2,128)(2,1)S(1)} %stack.391, bf16[1,1,512]{2,1,0:T(2,128)(2,1)S(1)} %stack.392, ...), dimensions={1} | concatenate | bytes 262144 | tf_op jit(solution)/shard_map/stack | solution.py:37
  118.3 0.0 all-gather.5.cloned.1.call-update
  118.3 0.0 reduce-scatter.2.cloned.1.call-start
  118.4 1.3 collective-permute-start.1
  119.7 0.0 copy-done.4
  119.7 0.0 copy-start.5
  119.7 0.0 copy-start.6
  119.7 0.0 copy-start.7
  119.7 0.0 copy-start.8
  119.7 0.0 copy-start.9
  119.7 0.0 copy-start.10
  119.7 0.0 copy-start.11
  119.7 0.0 copy-start.12
  119.7 0.0 copy-start.13
  119.8 0.0 copy-start.14
  119.8 0.0 copy-start.15
  119.8 0.0 copy-start.16
  119.8 0.0 copy-start.17
  119.8 0.0 copy-start.18
  119.8 5.8 %fusion.261 = f32[256,8192]{1,0:T(8,128)S(1)} fusion(bf16[8192,512]{1,0:T(8,128)(2,1)} %param.7, f32[256,512]{1,0:T(8,128)S(1)} %copy-done.4, bf16[256,512]{1,0:T(8,128)(2,1)S(1)} %copy-done), kind=kOutput, calls=%fused_computation.532 | convolution fusion | flops 2147876864 | bytes 17563648 | tf_op jit(solution)/shard_map/dot_general | solution.py:41
  125.6 0.0 collective-permute-done.1
  125.6 0.1 maximum_convert_fusion.1
  125.9 12.3 %fusion.134 = f32[256,512]{1,0:T(8,128)S(1)} fusion(f32[383,512]{1,0:T(8,128)S(1)} %maximum_convert_fusion.1, f32[512]{0:T(512)S(1)} %bitcast.392, f32[512]{0:T(512)S(1)} %bitcast.394, f32[512]{0:T(512)S(1)} %bitcast.294, f32[512]{0:T(512)S(1)} %bitcast.296, f32[512]{0:T(512)S(1)} %bitcast.298, f32[512]{0:T(512)S(1)} %bitcast.300, f32[512]{0:T(512)S(1)} %bitcast.302, ...), kind=kLoop, calls=%fused_computation.270 | loop fusion | flops 33423360 | bytes 67895296 | tf_op jit(solution)/shard_map/add | solution.py:28
  138.2 9.1 %convolution_add_fusion.1 = f32[256,8192]{1,0:T(8,128)} fusion(f32[256,8192]{1,0:T(8,128)S(1)} %fusion.261, bf16[8192,512]{1,0:T(8,128)(2,1)} %param.8, f32[256,512]{1,0:T(8,128)S(1)} %fusion.134, f32[256,512]{1,0:T(8,128)S(1)} %copy-done.3), kind=kOutput, calls=%fused_computation.129 | convolution fusion | flops 2149842944 | bytes 26214400 | tf_op jit(solution)/shard_map/dot_general | solution.py:41
  147.4 10.1 %fusion = bf16[256,8192]{1,0:T(8,128)(2,1)} fusion(f32[256,8192]{1,0:T(8,128)} %convolution_add_fusion.1, bf16[8192,512]{1,0:T(8,128)(2,1)} %param.9, f32[256,512]{1,0:T(8,128)S(1)} %fusion.134, f32[256,512]{1,0:T(8,128)S(1)} %copy-done.1), kind=kOutput, calls=%fused_computation.130 | convolution fusion | flops 2151940096 | bytes 22020096 | tf_op jit(solution)/shard_map/dot_general | solution.py:41
  157.5 0.0 reduce-scatter.2.cloned.1.call-update
  157.5 0.0 all-gather.5.cloned.1.call-done
  157.6 1.4 reduce_sum.1292
  158.9 0.7 convert_element_type.73
  159.7 78.8 %reduce-scatter.2.cloned.1.call-done = bf16[16,8192]{1,0:T(8,128)(2,1)} async-done(((bf16[256,8192]{1,0:T(8,128)(2,1)}), bf16[16,8192]{1,0:T(8,128)(2,1)}) %reduce-scatter.2.cloned.1.call-update) | async-done | bytes 262160 | tf_op jit(solution)/shard_map/reduce_scatter | solution.py:80
  (153 shorter events, 0.7 us)
Async XLA Ops:
  7.2 56.9 %all-gather.3.cloned.1.call-start = ((), (), s32[]{:S(2)}) async-start(), calls=%async_computation.1 | async-start | bytes 4456448 | tf_op jit(solution)/shard_map/all_gather | solution.py:51
  7.9 149.6 %all-gather.5.cloned.1.call-start = ((), (), s32[]{:S(2)}) async-start(), calls=%async_computation.3 | async-start | bytes 1179648 | tf_op jit(solution)/shard_map/all_gather | solution.py:6
  64.0 7.1 %copy-start.20 = (bf16[256,8192]{1,0:T(8,128)(2,1)S(1)}, bf16[256,8192]{1,0:T(8,128)(2,1)}, u32[]{:S(2)}) copy-start(bf16[256,8192]{1,0:T(8,128)(2,1)} %all-gather.3.cloned.1.call-done) | copy-start | bytes 12582916
  64.0 17.5 %slice-start = ((s8[8388608]{0:T(1024)(128)(4,1)}), s8[4194304]{0:T(1024)(128)(4,1)S(1)}, s32[]{:S(2)}) async-start(s8[8388608]{0:T(1024)(128)(4,1)} %bitcast.137), calls=%async_computation.4 | async-start | bytes 8388608
  71.2 6.8 %copy-start.2 = (f32[256,512]{1,0:T(8,128)}, f32[256,512]{1,0:T(8,128)S(1)}, u32[]{:S(2)}) copy-start(f32[256,512]{1,0:T(8,128)S(1)} %fusion.1) | copy-start | bytes 1572868
  71.2 10.4 %slice-start.1 = ((s8[8388608]{0:T(1024)(128)(4,1)}), s8[4194304]{0:T(1024)(128)(4,1)S(1)}, s32[]{:S(2)}) async-start(s8[8388608]{0:T(1024)(128)(4,1)} %bitcast.137), calls=%async_computation.5 | async-start | bytes 8388608
  78.0 3.4 %collective-permute-start = (bf16[127,512]{1,0:T(8,128)(2,1)S(1)}, bf16[127,512]{1,0:T(8,128)(2,1)S(1)}, u32[]{:S(2)}, u32[]{:S(2)}) collective-permute-start(bf16[127,512]{1,0:T(8,128)(2,1)S(1)} %slice.1812), channel_id=1, source_target_pairs={{0,16},{16,32},{32,48},{48,64},{64,80},{80,96},{96,112},{1,17},{17... | collective-permute-start | bytes 390152 | tf_op jit(solution)/shard_map/ppermute | solution.py:12
  81.6 16.6 %copy-start = (bf16[256,512]{1,0:T(8,128)(2,1)S(1)}, bf16[256,512]{1,0:T(8,128)(2,1)}, u32[]{:S(2)}) copy-start(bf16[256,512]{1,0:T(8,128)(2,1)} %param.11) | copy-start | bytes 786436
  104.5 15.1 %copy-start.4 = (f32[256,512]{1,0:T(8,128)S(1)}, f32[256,512]{1,0:T(8,128)}, u32[]{:S(2)}) copy-start(f32[256,512]{1,0:T(8,128)} %get-tuple-element.133) | copy-start | bytes 1572868
  118.3 120.1 %reduce-scatter.2.cloned.1.call-start = ((), (), s32[]{:S(2)}) async-start(), calls=%async_computation.2 | async-start | bytes 4456448 | tf_op jit(solution)/shard_map/reduce_scatter | solution.py:80
  118.4 7.2 %collective-permute-start.1 = (bf16[127,512]{1,0:T(8,128)(2,1)S(1)}, bf16[127,512]{1,0:T(8,128)(2,1)S(1)}, u32[]{:S(2)}, u32[]{:S(2)}) collective-permute-start(bf16[127,512]{1,0:T(8,128)(2,1)S(1)} %slice.1941), channel_id=1, source_target_pairs={{16,0},{32,16},{48,32},{64,48},{80,64},{96,80},{112,96},{17,1},{33... | collective-permute-start | bytes 390152 | tf_op jit(solution)/shard_map/ppermute | solution.py:12
  119.7 6.0 %copy-start.5 = (f32[1,512]{1,0:T(1,128)S(1)}, f32[1,512]{1,0:T(1,128)}, u32[]{:S(2)}) copy-start(f32[1,512]{1,0:T(1,128)} %get-tuple-element.247) | copy-start | bytes 6148
  119.7 6.0 %copy-start.6 = (f32[1,512]{1,0:T(1,128)S(1)}, f32[1,512]{1,0:T(1,128)}, u32[]{:S(2)}) copy-start(f32[1,512]{1,0:T(1,128)} %get-tuple-element.248) | copy-start | bytes 6148
  119.7 6.0 %copy-start.7 = (f32[1,512]{1,0:T(1,128)S(1)}, f32[1,512]{1,0:T(1,128)}, u32[]{:S(2)}) copy-start(f32[1,512]{1,0:T(1,128)} %get-tuple-element.249) | copy-start | bytes 6148
  119.7 6.0 %copy-start.8 = (f32[1,512]{1,0:T(1,128)S(1)}, f32[1,512]{1,0:T(1,128)}, u32[]{:S(2)}) copy-start(f32[1,512]{1,0:T(1,128)} %get-tuple-element.250) | copy-start | bytes 6148
  119.7 6.0 %copy-start.9 = (f32[1,512]{1,0:T(1,128)S(1)}, f32[1,512]{1,0:T(1,128)}, u32[]{:S(2)}) copy-start(f32[1,512]{1,0:T(1,128)} %get-tuple-element.251) | copy-start | bytes 6148
  119.7 6.0 %copy-start.10 = (f32[1,512]{1,0:T(1,128)S(1)}, f32[1,512]{1,0:T(1,128)}, u32[]{:S(2)}) copy-start(f32[1,512]{1,0:T(1,128)} %get-tuple-element.252) | copy-start | bytes 6148
  119.7 6.0 %copy-start.11 = (f32[1,512]{1,0:T(1,128)S(1)}, f32[1,512]{1,0:T(1,128)}, u32[]{:S(2)}) copy-start(f32[1,512]{1,0:T(1,128)} %get-tuple-element.253) | copy-start | bytes 6148
  119.7 6.0 %copy-start.12 = (f32[1,512]{1,0:T(1,128)S(1)}, f32[1,512]{1,0:T(1,128)}, u32[]{:S(2)}) copy-start(f32[1,512]{1,0:T(1,128)} %get-tuple-element.254) | copy-start | bytes 6148
  119.7 6.0 %copy-start.13 = (f32[1,512]{1,0:T(1,128)S(1)}, f32[1,512]{1,0:T(1,128)}, u32[]{:S(2)}) copy-start(f32[1,512]{1,0:T(1,128)} %get-tuple-element.255) | copy-start | bytes 6148
  119.8 6.0 %copy-start.14 = (f32[1,512]{1,0:T(1,128)S(1)}, f32[1,512]{1,0:T(1,128)}, u32[]{:S(2)}) copy-start(f32[1,512]{1,0:T(1,128)} %get-tuple-element.256) | copy-start | bytes 6148
  119.8 6.0 %copy-start.15 = (f32[1,512]{1,0:T(1,128)S(1)}, f32[1,512]{1,0:T(1,128)}, u32[]{:S(2)}) copy-start(f32[1,512]{1,0:T(1,128)} %get-tuple-element.257) | copy-start | bytes 6148
  119.8 6.0 %copy-start.16 = (f32[1,512]{1,0:T(1,128)S(1)}, f32[1,512]{1,0:T(1,128)}, u32[]{:S(2)}) copy-start(f32[1,512]{1,0:T(1,128)} %get-tuple-element.258) | copy-start | bytes 6148
  119.8 6.0 %copy-start.17 = (f32[1,512]{1,0:T(1,128)S(1)}, f32[1,512]{1,0:T(1,128)}, u32[]{:S(2)}) copy-start(f32[1,512]{1,0:T(1,128)} %get-tuple-element.259) | copy-start | bytes 6148
  119.8 6.0 %copy-start.18 = (f32[1,512]{1,0:T(1,128)S(1)}, f32[1,512]{1,0:T(1,128)}, u32[]{:S(2)}) copy-start(f32[1,512]{1,0:T(1,128)} %get-tuple-element.260) | copy-start | bytes 6148
  119.8 6.0 %copy-start.19 = (f32[1,512]{1,0:T(1,128)S(1)}, f32[1,512]{1,0:T(1,128)}, u32[]{:S(2)}) copy-start(f32[1,512]{1,0:T(1,128)} %get-tuple-element.261) | copy-start | bytes 6148
  125.8 12.4 %copy-start.3 = (f32[256,512]{1,0:T(8,128)S(1)}, f32[256,512]{1,0:T(8,128)}, u32[]{:S(2)}) copy-start(f32[256,512]{1,0:T(8,128)} %copy-done.2) | copy-start | bytes 1572868
  138.2 9.2 %copy-start.1 = (f32[256,512]{1,0:T(8,128)S(1)}, f32[256,512]{1,0:T(8,128)}, u32[]{:S(2)}) copy-start(f32[256,512]{1,0:T(8,128)} %get-tuple-element.263) | copy-start | bytes 1572868
Sparse Core Ops, SparseCore 0:
  10.1 53.8 all-gather.2
  118.4 26.1 all-gather.4
  157.6 80.7 reduce-scatter.1
